TPU v7x, 512 devices: a whole 4x8x8 slice. The times are simulated.
512 devices in a mesh: gx: 4 (over x), gy: 16 (over z, core), gz: 8 (over y).
Axes of the slice: x: 4, y: 8, z: 8, core: 2. Of those that a mesh axis runs over, the one named last changes fastest.
Arguments:
- features: bfloat16 [65536, 25, 128], P(('gx', 'gy', 'gz')), may hold values from -6 to 6
- positions: bfloat16 [3, 65536], P(None, ('gx', 'gy', 'gz')), may hold values from 0 to 4
- probe_positions: float32 [3, 131072], P(None, ('gx', 'gy', 'gz')), may hold values from 0 to 4
- neighbours: int32 [65536, 20], P(('gx', 'gy', 'gz')), may hold values from 0 to 235
- routes: int32 [65536, 1], P(('gx', 'gy', 'gz')), may hold values from 0 to 127; in each aligned block of 128 rows (0 to 127, 128 to 255, ...) at most 2 rows name the same one
- pattern: int32 [1024, 128], P(('gx', 'gy', 'gz')), may hold values 0 or 1
- charge_index: int32 [1], replicated, may hold values from 0 to 7
- charge_table: bfloat16 [8, 128], replicated, may hold values from -6 to 6
- w_radial_in: bfloat16 [8, 64], replicated, may hold values from -2 to 2
- w_radial_out: bfloat16 [64, 1280], replicated, may hold values from -0.75 to 0.75
- w_mix: bfloat16 [5, 128, 128], replicated, may hold values from -0.5 to 0.5
- w_self: bfloat16 [5, 128, 128], replicated, may hold values from -0.5 to 0.5
- w_gate: bfloat16 [128, 512], replicated, may hold values from -0.5 to 0.5
- w_read: bfloat16 [8, 5, 128], replicated, may hold values from -0.5 to 0.5
Outputs:
- atoms_out: bfloat16 [65536, 25, 128], P(('gx', 'gy', 'gz'))
- density: float32 [131072], P(('gx', 'gy', 'gz'))
Inputs may be any that keep to these rules, and one draw needn't show every extreme that they name: `routes`: A tile number t is gy index times 8 plus gz index within the atom's gx plane; the rows of one box name each tile at most 2 times and name different tiles in one row.
All inputs are finite; a program needn't handle non-finite values. No bound on the sum of `pattern` on one device may be relied on, other than what follows from the above.
Results may differ from a plain program's by a relative error of at most 0.0031.
Values may be sent and summed in bfloat16 or wider, within the bound.
A program may use at most 64 MiB of HBM per device.

v0:
```python
import math

import jax
import jax.numpy as jnp
from jax import lax
from jax.sharding import PartitionSpec as P

PB = 128


CUTOFF = 8.0
WIDTH_R = 0.75
REACH = 6.0
FLOOR = 0.25


def extended(cells, sides, width):
    for axis, dim in sides:
        count = lax.axis_size(axis)
        head = lax.slice_in_dim(cells, 0, width, axis=dim)
        tail = lax.slice_in_dim(cells, cells.shape[dim] - width, cells.shape[dim], axis=dim)
        cells = jnp.concatenate(
            [
                lax.ppermute(tail, axis, [(i, (i + 1) % count) for i in range(count)]),
                cells,
                lax.ppermute(head, axis, [((i + 1) % count, i) for i in range(count)]),
            ],
            axis=dim,
        )
    return cells


def harmonics(comp_x, comp_y, comp_z):
    sq_x = comp_x * comp_x
    sq_y = comp_y * comp_y
    sq_z = comp_z * comp_z
    return jnp.stack(
        [
            jnp.ones_like(comp_x),
            math.sqrt(3.0) * comp_y,
            math.sqrt(3.0) * comp_z,
            math.sqrt(3.0) * comp_x,
            math.sqrt(15.0) * comp_x * comp_y,
            math.sqrt(15.0) * comp_y * comp_z,
            0.5 * math.sqrt(5.0) * (3.0 * sq_z - 1.0),
            math.sqrt(15.0) * comp_x * comp_z,
            0.5 * math.sqrt(15.0) * (sq_x - sq_y),
            math.sqrt(35.0 / 8.0) * comp_y * (3.0 * sq_x - sq_y),
            math.sqrt(105.0) * comp_x * comp_y * comp_z,
            math.sqrt(21.0 / 8.0) * comp_y * (5.0 * sq_z - 1.0),
            0.5 * math.sqrt(7.0) * comp_z * (5.0 * sq_z - 3.0),
            math.sqrt(21.0 / 8.0) * comp_x * (5.0 * sq_z - 1.0),
            0.5 * math.sqrt(105.0) * comp_z * (sq_x - sq_y),
            math.sqrt(35.0 / 8.0) * comp_x * (sq_x - 3.0 * sq_y),
            1.5 * math.sqrt(35.0) * comp_x * comp_y * (sq_x - sq_y),
            1.5 * math.sqrt(17.5) * comp_y * comp_z * (3.0 * sq_x - sq_y),
            1.5 * math.sqrt(5.0) * comp_x * comp_y * (7.0 * sq_z - 1.0),
            1.5 * math.sqrt(2.5) * comp_y * comp_z * (7.0 * sq_z - 3.0),
            0.375 * (35.0 * sq_z * sq_z - 30.0 * sq_z + 3.0),
            1.5 * math.sqrt(2.5) * comp_x * comp_z * (7.0 * sq_z - 3.0),
            0.75 * math.sqrt(5.0) * (sq_x - sq_y) * (7.0 * sq_z - 1.0),
            1.5 * math.sqrt(17.5) * comp_x * comp_z * (sq_x - 3.0 * sq_y),
            0.375 * math.sqrt(35.0) * (sq_x * sq_x - 6.0 * sq_x * sq_y + sq_y * sq_y),
        ]
    )


def radial_basis(distance, functions):
    centres = jnp.arange(functions).astype(jnp.float32) * (REACH / (functions - 1))
    bcast_shape = (functions,) + (1,) * distance.ndim
    envelope = jnp.square(1.0 - jnp.square(distance / CUTOFF))
    return (
        jnp.exp(-jnp.square((distance[None] - centres.reshape(bcast_shape)) / WIDTH_R))
        * envelope[None]
    )


def geometry(offset_vec):
    distance = jnp.sqrt(jnp.sum(offset_vec * offset_vec, axis=0))
    direction = offset_vec / jnp.maximum(distance, FLOOR)[None]
    return (distance, harmonics(direction[0], direction[1], direction[2]))


def degree_of(component):
    return int(math.isqrt(component))


def embed_flat(flat_feats, charge_index, charge_table, channels):
    levels = charge_table.shape[0]
    chosen = (jnp.arange(levels) == charge_index[0]).astype(jnp.float32)
    charge_shift = jnp.sum(chosen[:, None] * charge_table.astype(jnp.float32), axis=0)
    scalar = (flat_feats[:, :channels].astype(jnp.float32) + charge_shift[None, :]).astype(
        jnp.bfloat16
    )
    return jnp.concatenate([scalar, flat_feats[:, channels:]], axis=1)


def aggregate_flat(
    feats_all, pos_all, neighbours, own_pos, w_radial_in, w_radial_out, channels, degrees
):
    row_count, fanout = neighbours.shape
    components = degrees * degrees
    block_rows = 16

    def one_block(inputs):
        index_block, centre = inputs
        flat_index = index_block.reshape(-1)
        gathered = jnp.take(feats_all, flat_index, axis=0)
        offset_vec = (jnp.take(pos_all, flat_index, axis=0) - jnp.repeat(centre, fanout, axis=0)).T
        distance, angular = geometry(offset_vec)
        radial_in = radial_basis(distance, w_radial_in.shape[0]).T.astype(jnp.bfloat16)
        hidden = jax.nn.silu(
            jnp.dot(radial_in, w_radial_in, preferred_element_type=jnp.float32)
        ).astype(jnp.bfloat16)
        radial = jnp.dot(hidden, w_radial_out, preferred_element_type=jnp.float32)
        scalar_vals = gathered[:, :channels].astype(jnp.float32)
        pieces = []
        for component in range(components):
            degree = degree_of(component)
            same_path = radial[:, degree * channels : (degree + 1) * channels]
            cross_path = radial[
                :, (degrees + degree) * channels : (degrees + degree + 1) * channels
            ]
            values = gathered[:, component * channels : (component + 1) * channels].astype(
                jnp.float32
            )
            pieces.append(
                same_path * values + cross_path * scalar_vals * angular[component][:, None]
            )
        message = jnp.concatenate(pieces, axis=1)
        return jnp.sum(message.reshape(block_rows, fanout, components * channels), axis=1) * (
            1.0 / math.sqrt(fanout)
        )

    result = lax.map(
        one_block,
        (
            neighbours.reshape(row_count // block_rows, block_rows, fanout),
            own_pos.reshape(row_count // block_rows, block_rows, 3),
        ),
    )
    return result.reshape(row_count, components * channels).astype(jnp.bfloat16)


def update_flat(embedded, aggregated, w_mix, w_self, w_gate, channels, degrees):
    components = degrees * degrees
    gate_values = jax.nn.sigmoid(
        jnp.dot(aggregated[:, :channels], w_gate, preferred_element_type=jnp.float32)
    )
    pieces = []
    for component in range(components):
        degree = degree_of(component)
        agg_part = aggregated[:, component * channels : (component + 1) * channels]
        own_part = embedded[:, component * channels : (component + 1) * channels]
        mixed_term = jnp.dot(agg_part, w_mix[degree], preferred_element_type=jnp.float32)
        mixed_term = mixed_term + jnp.dot(
            own_part, w_self[degree], preferred_element_type=jnp.float32
        )
        residual_part = own_part.astype(jnp.float32)
        if degree == 0:
            pieces.append(residual_part + jax.nn.silu(mixed_term))
        else:
            pieces.append(
                residual_part
                + mixed_term * gate_values[:, (degree - 1) * channels : degree * channels]
            )
    return jnp.concatenate(pieces, axis=1).astype(jnp.bfloat16)


def readout_flat(flat_feats, w_read, channels, degrees):
    components = degrees * degrees
    pieces = []
    for component in range(components):
        degree = degree_of(component)
        part = flat_feats[:, component * channels : (component + 1) * channels]
        pieces.append(jnp.dot(part, w_read[:, degree, :].T, preferred_element_type=jnp.float32))
    return jnp.stack(pieces, axis=2)


def slot_rows(routes, dests, capacity):
    row_count, cover_count = routes.shape
    flat_dest = routes.reshape(-1)
    onehot = (flat_dest[:, None] == jnp.arange(dests)[None, :]).astype(jnp.int32)
    rank_in_dest = jnp.sum((jnp.cumsum(onehot, axis=0) - 1) * onehot, axis=1)
    slot_index = flat_dest * capacity + rank_in_dest
    source_row = jnp.arange(row_count * cover_count) // cover_count
    return jnp.full((dests * capacity,), row_count, jnp.int32).at[slot_index].set(source_row)


def density_tile(probe_pos, pattern, slot_pos, slot_coeffs, capacity, probe_block):
    slot_count = slot_pos.shape[0]
    probe_count = probe_pos.shape[1]
    span = 128
    keep_mask = jnp.repeat(
        jnp.repeat(pattern.astype(jnp.float32), probe_block, axis=0), capacity, axis=1
    )

    def one_span(total, start):
        where_pos = lax.dynamic_slice_in_dim(slot_pos, start, span, 0)
        coeffs = lax.dynamic_slice_in_dim(slot_coeffs, start, span, 0)
        keep = lax.dynamic_slice_in_dim(keep_mask, start, span, 1)
        offset_vec = probe_pos[:, :, None] - where_pos.T[:, None, :]
        distance, angular = geometry(offset_vec)
        radial_in = radial_basis(distance, coeffs.shape[1])
        contracted = jnp.einsum("lps,sbl->bps", angular, coeffs, precision=lax.Precision.HIGHEST)
        return (total + jnp.sum(jnp.sum(radial_in * contracted, axis=0) * keep, axis=1), None)

    starts = jnp.arange(0, slot_count, span)
    total, unused = lax.scan(one_span, jnp.zeros((probe_count,), jnp.float32), starts)
    return total * (1.0 / math.sqrt(slot_count))


def per_device(
    features,
    positions,
    probe_positions,
    neighbours,
    routes,
    pattern,
    charge_index,
    charge_table,
    w_radial_in,
    w_radial_out,
    w_mix,
    w_self,
    w_gate,
    w_read,
):
    per_dev, components, channels = features.shape
    degrees = w_mix.shape[0]
    width = components * channels
    rim = per_dev // 32
    embedded = embed_flat(features.reshape(per_dev, width), charge_index, charge_table, channels)
    atom_pos = positions.astype(jnp.float32).T
    rim_coords = jnp.pad(positions[:, :rim].T, ((0, 0), (0, channels - 3)))
    rim_block = jnp.concatenate([embedded[:rim], rim_coords], axis=1)[None, None, None]
    grown = extended(rim_block, (("gx", 0), ("gy", 1), ("gz", 2)), 1)
    grown = grown.reshape(27 * rim, width + channels)
    feats_all = jnp.concatenate([embedded, grown[:, :width]], axis=0)
    pos_all = jnp.concatenate([atom_pos, grown[:, width : width + 3].astype(jnp.float32)], axis=0)
    aggregated = aggregate_flat(
        feats_all, pos_all, neighbours, atom_pos, w_radial_in, w_radial_out, channels, degrees
    )
    updated = update_flat(embedded, aggregated, w_mix, w_self, w_gate, channels, degrees)
    size_y = lax.axis_size("gy")
    size_z = lax.axis_size("gz")
    dests = size_y * size_z
    capacity = max(2, 2 * per_dev * routes.shape[1] // dests)
    slot_table = slot_rows(routes, dests, capacity)
    padded_pos = jnp.concatenate([positions.T, jnp.zeros((1, 3), jnp.bfloat16)], axis=0)
    outgoing_pos = jnp.take(padded_pos, slot_table, axis=0).reshape(dests, capacity, 3)
    padded_feats = jnp.concatenate([updated, jnp.zeros((1, width), jnp.bfloat16)], axis=0)
    outgoing = jnp.take(padded_feats, slot_table, axis=0).reshape(dests, capacity, width)
    arrived_feats, arrived_pos = (
        lax.all_to_all(outgoing, ("gy", "gz"), split_axis=0, concat_axis=0, tiled=True),
        lax.all_to_all(outgoing_pos, ("gy", "gz"), split_axis=0, concat_axis=0, tiled=True),
    )
    slot_coeffs = readout_flat(arrived_feats.reshape(-1, width), w_read, channels, degrees)
    slot_pos = arrived_pos.reshape(-1, 3).astype(jnp.float32)
    density = density_tile(probe_positions, pattern, slot_pos, slot_coeffs, capacity, PB)
    return (updated.reshape(per_dev, components, channels), density)


def solution(mesh):
    in_specs = (
        P(("gx", "gy", "gz"), None, None),
        P(None, ("gx", "gy", "gz")),
        P(None, ("gx", "gy", "gz")),
        P(("gx", "gy", "gz"), None),
        P(("gx", "gy", "gz"), None),
        P(("gx", "gy", "gz"), None),
        P(),
        P(),
        P(),
        P(),
        P(),
        P(),
        P(),
        P(),
    )
    out_specs = (P(("gx", "gy", "gz"), None, None), P(("gx", "gy", "gz")))
    return jax.shard_map(
        per_device, mesh=mesh, in_specs=in_specs, out_specs=out_specs, check_vma=False
    )
```

profile of v0, /device:TPU:1, one launch (start us, length us, event | category | flops | bytes accessed | tf_op | source)
XLA Modules:
  0.0 498.7 jit_solution(10444093543187960461)
XLA Ops:
  4.7 3.9 collective-permute-start
  13.6 3.8 collective-permute-start.2
  24.6 3.8 collective-permute-start.5
  29.3 16.2 %all-to-all-start = ((bf16[128,2,3]{2,1,0:T(2,128)(2,1)}), bf16[128,2,3]{2,1,0:T(2,128)(2,1)S(1)}, u32[]{:S(2)}, u32[]{:S(2)}) async-start(bf16[128,2,3]{2,1,0:T(2,128)(2,1)} %broadcast_select_fusion.2), calls=%async_computation | async-start | bytes 131072 | tf_op jit(solution)/shard_map/all_to_all | solution.py:256
  50.7 315.5 %while.27 = (s32[]{:T(128)}, bf16[8,16,3200]{2,1,0:T(8,128)(2,1)}, s32[8,16,20]{2,1,0:T(8,128)}, f32[236,3]{1,0:T(8,128)S(1)}, f32[8,16,3]{1,2,0:T(4,128)S(1)}, ...) while((s32[]{:T(128)}, bf16[8,16,3200]{2,1,0:T(8,128)(2,1)}, ...), condition=%wide.region_4.5_spmd, body=%wide.region_1.4_spmd.sunk | while | flops 59832080 | bytes 38572412 | solution.py:135
  55.9 3.6 gather_fusion.1
  81.5 5.0 reshape.764
  95.3 3.6 gather_fusion.1
  121.0 5.0 reshape.764
  134.7 3.6 gather_fusion.1
  160.4 5.0 reshape.764
  174.2 3.6 gather_fusion.1
  199.8 5.0 reshape.764
  239.3 5.0 reshape.764
  278.7 5.0 reshape.764
  292.5 3.6 gather_fusion.1
  318.2 5.0 reshape.764
  331.9 3.6 gather_fusion.1
  357.6 5.0 reshape.764
  405.9 13.7 %all-to-all-start.1 = ((bf16[128,2,3200]{2,1,0:T(2,128)(2,1)}), bf16[128,2,3200]{2,1,0:T(2,128)(2,1)S(1)}, u32[]{:S(2)}, u32[]{:S(2)}) async-start(bf16[128,2,3200]{2,1,0:T(2,128)(2,1)} %broadcast_select_fusion.1), calls=%async_computation.1 | async-start | bytes 3276800 | tf_op jit(solution)/shard_map/all_to_all | solution.py:255
  422.5 40.0 %all-to-all-done.1 = bf16[128,2,3200]{2,1,0:T(2,128)(2,1)S(1)} async-done(((bf16[128,2,3200]{2,1,0:T(2,128)(2,1)}), bf16[128,2,3200]{2,1,0:T(2,128)(2,1)S(1)}, u32[]{:S(2)}, u32[]{:S(2)}) %all-to-all-start.1) | async-done | bytes 1638432 | tf_op jit(solution)/shard_map/all_to_all | solution.py:255
  467.6 30.6 %while.28 = (s32[]{:T(128)}, f32[256]{0:T(256)S(1)}, f32[3,256]{1,0:T(4,128)S(1)}, s32[2]{0:T(128)S(1)}, f32[256,3]{0,1:T(4,128)S(1)}, /*index=5*/f32[256,8,25]{...) while((s32[]{:T(128)}, f32[256]{0:T(256)S(1)}, f32[3,256]{1,0:T(4,128)S(1)}, ...), condition=%wide.region_12.13_spmd.clone, body=%wide.region_8.12_spmd.clone.sunk | while | flops 84574480 | bytes 23335292 | solution.py:209
  478.2 4.6 fusion.411
  493.5 4.6 fusion.411
  (742 shorter events, 339.1 us)
Async XLA Ops:
  0.6 390.4 %copy-start = (bf16[128,512]{1,0:T(8,128)(2,1)S(1)}, bf16[128,512]{1,0:T(8,128)(2,1)}, u32[]{:S(2)}) copy-start(bf16[128,512]{1,0:T(8,128)(2,1)} %param.30) | copy-start | bytes 393220
  0.7 11.2 %copy-start.19 = (s32[128,1]{0,1:T(1,128)S(1)}, s32[128,1]{0,1:T(1,128)}, u32[]{:S(2)}) copy-start(s32[128,1]{0,1:T(1,128)} %param.22) | copy-start | bytes 1540
  2.4 11.0 %copy-start.1 = (bf16[128,25,128]{0,2,1:T(8,128)(2,1)}, bf16[128,25,128]{0,2,1:T(8,128)(2,1)S(1)}, u32[]{:S(2)}) copy-start(bf16[128,25,128]{0,2,1:T(8,128)(2,1)S(1)} %copy.105) | copy-start | bytes 2457604
  2.4 43.2 %copy-start.17 = (s32[128,20]{0,1:T(8,128)S(1)}, s32[128,20]{0,1:T(8,128)}, u32[]{:S(2)}) copy-start(s32[128,20]{0,1:T(8,128)} %param.21) | copy-start | bytes 30724
  4.7 8.8 %collective-permute-start = (bf16[1,1,1,4,3328]{4,3,2,1,0:T(4,128)(2,1)S(1)}, bf16[1,1,1,4,3328]{4,3,2,1,0:T(4,128)(2,1)S(1)}, u32[]{:S(2)}, u32[]{:S(2)}) collective-permute-start(bf16[1,1,1,4,3328]{4,3,2,1,0:T(4,128)(2,1)S(1)} %fusion.281), channel_id=1, source_target_pairs={{0,128},{128,256},{256,384},{384,0},{1,129},{129,257},{257,385},{3... | collective-permute-start | bytes 79880 | tf_op jit(solution)/shard_map/ppermute | solution.py:24
  8.6 4.9 collective-permute-start.1
  13.5 33.0 %copy-start.13 = (pred[128,2]{1,0:T(8,128)(4,1)}, pred[128,2]{1,0:T(8,128)(4,1)S(1)}, u32[]{:S(2)}) copy-start(pred[128,2]{1,0:T(8,128)(4,1)S(1)} %broadcast_in_dim.104) | copy-start | bytes 772
  13.6 7.7 %collective-permute-start.2 = (bf16[3,1,1,4,3328]{4,3,2,1,0:T(4,128)(2,1)S(1)}, bf16[3,1,1,4,3328]{4,3,2,1,0:T(4,128)(2,1)S(1)}, u32[]{:S(2)}, u32[]{:S(2)}) collective-permute-start(bf16[3,1,1,4,3328]{4,3,2,1,0:T(4,128)(2,1)S(1)} %pad_maximum_fusion.4), channel_id=1, source_target_pairs={{0,8},{8,16},{16,24},{24,32},{32,40},{40,48},{48,56},{56,64},{64,7... | collective-permute-start | bytes 239624 | tf_op jit(solution)/shard_map/ppermute | solution.py:24
  17.4 3.9 collective-permute-start.3
  20.4 28.2 %copy-start.18 = (s32[1024]{0:T(1024)}, s32[1024]{0:T(1024)S(1)}, u32[]{:S(2)}) copy-start(s32[1024]{0:T(1024)S(1)} %pad_clamp_fusion.1) | copy-start | bytes 12292
  21.5 24.9 %collective-permute-start.4 = (bf16[3,3,1,4,3328]{4,3,2,1,0:T(4,128)(2,1)S(1)}, bf16[3,3,1,4,3328]{4,3,2,1,0:T(4,128)(2,1)S(1)}, u32[]{:S(2)}, u32[]{:S(2)}) collective-permute-start(bf16[3,3,1,4,3328]{4,3,2,1,0:T(4,128)(2,1)S(1)} %pad_maximum_fusion.3), channel_id=1, source_target_pairs={{0,1},{1,2},{2,3},{3,4},{4,5},{5,6},{6,7},{7,0},{8,9},{9,10},{10,1... | collective-permute-start | bytes 718856 | tf_op jit(solution)/shard_map/ppermute | solution.py:24
  24.6 21.8 %collective-permute-start.5 = (bf16[3,3,1,4,3328]{4,3,2,1,0:T(4,128)(2,1)S(1)}, bf16[3,3,1,4,3328]{4,3,2,1,0:T(4,128)(2,1)S(1)}, u32[]{:S(2)}, u32[]{:S(2)}) collective-permute-start(bf16[3,3,1,4,3328]{4,3,2,1,0:T(4,128)(2,1)S(1)} %pad_maximum_fusion.3), channel_id=1, source_target_pairs={{1,0},{2,1},{3,2},{4,3},{5,4},{6,5},{7,6},{0,7},{9,8},{10,9},{11,1... | collective-permute-start | bytes 718856 | tf_op jit(solution)/shard_map/ppermute | solution.py:26
  29.3 376.6 %all-to-all-start = ((bf16[128,2,3]{2,1,0:T(2,128)(2,1)}), bf16[128,2,3]{2,1,0:T(2,128)(2,1)S(1)}, u32[]{:S(2)}, u32[]{:S(2)}) async-start(bf16[128,2,3]{2,1,0:T(2,128)(2,1)} %broadcast_select_fusion.2), calls=%async_computation | async-start | bytes 131072 | tf_op jit(solution)/shard_map/all_to_all | solution.py:256
  366.2 25.8 %copy-start.3 = (bf16[5,128,128]{2,1,0:T(8,128)(2,1)S(1)}, bf16[5,128,128]{2,1,0:T(8,128)(2,1)}, u32[]{:S(2)}) copy-start(bf16[5,128,128]{2,1,0:T(8,128)(2,1)} %param.29) | copy-start | bytes 491524
  366.3 26.1 %copy-start.2 = (bf16[128,25,128]{0,2,1:T(8,128)(2,1)S(1)}, bf16[128,25,128]{0,2,1:T(8,128)(2,1)}, u32[]{:S(2)}) copy-start(bf16[128,25,128]{0,2,1:T(8,128)(2,1)} %copy-done.1) | copy-start | bytes 2457604
  403.1 16.5 %copy-start.21 = (s32[2,128]{1,0:T(2,128)S(1)}, s32[2,128]{1,0:T(2,128)}, u32[]{:S(2)}) copy-start(s32[2,128]{1,0:T(2,128)} %param.23) | copy-start | bytes 3076
  403.1 18.0 %copy-start.8 = (bf16[128,25,128]{0,2,1:T(8,128)(2,1)S(1)}, bf16[128,25,128]{0,2,1:T(8,128)(2,1)}, u32[]{:S(2)}) copy-start(bf16[128,25,128]{0,2,1:T(8,128)(2,1)} %copy-done.7) | copy-start | bytes 2457604
  405.9 56.6 %all-to-all-start.1 = ((bf16[128,2,3200]{2,1,0:T(2,128)(2,1)}), bf16[128,2,3200]{2,1,0:T(2,128)(2,1)S(1)}, u32[]{:S(2)}, u32[]{:S(2)}) async-start(bf16[128,2,3200]{2,1,0:T(2,128)(2,1)} %broadcast_select_fusion.1), calls=%async_computation.1 | async-start | bytes 3276800 | tf_op jit(solution)/shard_map/all_to_all | solution.py:255
  419.6 43.6 %copy-start.22 = (bf16[8,5,128]{2,0,1:T(8,128)(2,1)S(1)}, bf16[8,5,128]{2,0,1:T(8,128)(2,1)}, u32[]{:S(2)}) copy-start(bf16[8,5,128]{2,0,1:T(8,128)(2,1)} %param.31) | copy-start | bytes 30724
  421.1 46.5 %copy-start.9 = (f32[3,256]{1,0:T(4,128)S(1)}, f32[3,256]{1,0:T(4,128)}, u32[]{:S(2)}) copy-start(f32[3,256]{1,0:T(4,128)} %param.20) | copy-start | bytes 9220
  475.7 7.1 %copy-start.4 = (f32[256,256]{0,1:T(8,128)S(1)}, f32[256,256]{0,1:T(8,128)}, u32[]{:S(2)}) copy-start(f32[256,256]{0,1:T(8,128)} %get-tuple-element.749) | copy-start | bytes 786436 | tf_op jit(solution)/shard_map/while
  476.8 6.1 %copy-start.24 = (s32[2]{0:T(128)S(1)}, s32[2]{0:T(128)}, u32[]{:S(2)}) copy-start(s32[2]{0:T(128)} %copy-done.23) | copy-start | bytes 28 | tf_op jit(solution)/shard_map/while
  491.0 7.1 %copy-start.4 = (f32[256,256]{0,1:T(8,128)S(1)}, f32[256,256]{0,1:T(8,128)}, u32[]{:S(2)}) copy-start(f32[256,256]{0,1:T(8,128)} %get-tuple-element.749) | copy-start | bytes 786436 | tf_op jit(solution)/shard_map/while
  492.1 6.1 %copy-start.24 = (s32[2]{0:T(128)S(1)}, s32[2]{0:T(128)}, u32[]{:S(2)}) copy-start(s32[2]{0:T(128)} %copy-done.23) | copy-start | bytes 28 | tf_op jit(solution)/shard_map/while
  (48 other events, 125.3 us)
where the time goes:
time: 503 us; the launch traced here: 499 us
  other arithmetic  226 us (45%)
  local copies, waits for them, and re-layouts  118 us (23%)
  matrix products  56.9 us (11%)
  starting transfers between devices  50.7 us (10%)
  waiting for transfers between devices  40.1 us (8%)
  loops' own time  5.25 us (1%)
    while x238, other arithmetic  155 us
    all_to_all x1, waiting for transfers between devices, per_device(): lax.all_to_all(outgoing, ('gy', 'gz'), split_axis=0, concat_axis=0, tiled...  40 us
    reshape x8, local copies, waits for them, and re-layouts, one_block(): message.reshape(block_rows, fanout, components * channels)  39.7 us
    gather x8, local copies, waits for them, and re-layouts, one_block(): gathered = jnp.take(feats_all, flat_index, axis=0)  29.1 us
    dot_general x25, matrix products, update_flat(): jnp.dot(agg_part, w_mix[degree], preferred_element_type=jnp.float32)  24.7 us
    reduce_sum x8, other arithmetic, one_block(): jnp.sum(message.reshape(block_rows, fanout, components * channels), axis=1)  24.1 us
    all_to_all x1, starting transfers between devices, per_device(): lax.all_to_all(outgoing_pos, ('gy', 'gz'), split_axis=0, concat_axis=0, t...  16.2 us
    select_n x8, other arithmetic, one_block(): gathered = jnp.take(feats_all, flat_index, axis=0)  14.8 us
  transfers between devices with their start and end apart: 8, of which 2 were waited for; matrix products, arithmetic and copies ran while one was open for 73% of the time, Pallas kernels for 0%

commit v1 on v0

v1 whole, which is shorter than its diff:
```python
import functools, math
import jax
import jax.numpy as jnp
from jax import lax
from jax.experimental import pallas as pl
from jax.experimental.pallas import tpu as pltpu
from jax.sharding import PartitionSpec as P

F32 = jnp.float32
BF16 = jnp.bfloat16
CUTOFF = 8.0
WIDTH_R = 0.75
REACH = 6.0
FLOOR = 0.25
N_FUN = 8
DEG = 5
COMP = 25
CH = 128
ATOMS = 128
FAN = 20
GROUP = 8
N_GROUP = 16
EDGE = GROUP * FAN
CHUNK = 4
MAXN = 256


def degree_of(component):
    return int(math.isqrt(component))


def harmonics(x, y, z):
    xx, yy, zz = x * x, y * y, z * z
    c = math.sqrt
    return [
        jnp.ones_like(x),
        c(3.0) * y,
        c(3.0) * z,
        c(3.0) * x,
        c(15.0) * x * y,
        c(15.0) * y * z,
        0.5 * c(5.0) * (3.0 * zz - 1.0),
        c(15.0) * x * z,
        0.5 * c(15.0) * (xx - yy),
        c(35.0 / 8.0) * y * (3.0 * xx - yy),
        c(105.0) * x * y * z,
        c(21.0 / 8.0) * y * (5.0 * zz - 1.0),
        0.5 * c(7.0) * z * (5.0 * zz - 3.0),
        c(21.0 / 8.0) * x * (5.0 * zz - 1.0),
        0.5 * c(105.0) * z * (xx - yy),
        c(35.0 / 8.0) * x * (xx - 3.0 * yy),
        1.5 * c(35.0) * x * y * (xx - yy),
        1.5 * c(17.5) * y * z * (3.0 * xx - yy),
        1.5 * c(5.0) * x * y * (7.0 * zz - 1.0),
        1.5 * c(2.5) * y * z * (7.0 * zz - 3.0),
        0.375 * (35.0 * zz * zz - 30.0 * zz + 3.0),
        1.5 * c(2.5) * x * z * (7.0 * zz - 3.0),
        0.75 * c(5.0) * (xx - yy) * (7.0 * zz - 1.0),
        1.5 * c(17.5) * x * z * (xx - 3.0 * yy),
        0.375 * c(35.0) * (xx * xx - 6.0 * xx * yy + yy * yy),
    ]


def radial_funs(d):
    q = d * (1.0 / CUTOFF)
    env = 1.0 - q * q
    env = env * env
    out = []
    for b in range(N_FUN):
        v = (d - b * (REACH / (N_FUN - 1))) * (1.0 / WIDTH_R)
        out.append(jnp.exp(-(v * v)) * env)
    return out


def geometry(dx, dy, dz):
    d = jnp.sqrt(dx * dx + dy * dy + dz * dz)
    inv = 1.0 / jnp.maximum(d, FLOOR)
    return d, dx * inv, dy * inv, dz * inv


def iota(shape, dim):
    return lax.broadcasted_iota(jnp.int32, shape, dim)


def dot(a, b, dims=None):
    if dims is None:
        dims = (((1,), (0,)), ((), ()))
    return lax.dot_general(a, b, dims, preferred_element_type=F32)


NT = (((1,), (1,)), ((), ()))
TN = (((0,), (0,)), ((), ()))


def atom_kernel(
    ci_ref, nbr_ref, routes_ref, pos_ref, feats_ref, ghost_ref, table_ref, w_in_ref, w_out_ref,
    w_mix_ref, w_self_ref, w_gate_ref, w_read_ref, upd_ref, send_ref,
    f_ref, oh_ref, xyz_ref, ys_ref, bas_ref, r_ref, agg_ref,
):
    lvl = iota((8, CH), 0)
    shift = jnp.sum(
        jnp.where(lvl == ci_ref[0], table_ref[...].astype(F32), 0.0), axis=0, keepdims=True
    )
    keep = iota((112, CH), 0) < 108
    zero16 = jnp.zeros((16, CH), BF16)
    for m in range(COMP):
        own = feats_ref[m]
        gh = ghost_ref[m].astype(F32)
        if m == 0:
            own = (own.astype(F32) + shift).astype(BF16)
            gh = gh + shift
        gh = jnp.where(keep, gh, 0.0).astype(BF16)
        lanes = slice(m * CH, (m + 1) * CH)
        f_ref[0:ATOMS, lanes] = own
        f_ref[ATOMS : ATOMS + 112, lanes] = gh
        f_ref[ATOMS + 112 :, lanes] = zero16
    nbr = nbr_ref[...]
    col = iota((ATOMS, MAXN), 1)
    for k in range(0, FAN, 2):
        halves = []
        for kk in (k, k + 1):
            hot = jnp.where(nbr[:, kk : kk + 1] == col, 1.0, 0.0)
            halves.append(hot.reshape(N_GROUP, GROUP, MAXN))
        oh_ref[:, k * GROUP : (k + 2) * GROUP, :] = jnp.concatenate(halves, axis=1).astype(BF16)
    pos = pos_ref[...].astype(F32)
    gpos = jnp.where(keep, ghost_ref[COMP].astype(F32), 0.0)
    gpos_t = jnp.concatenate([gpos, jnp.zeros((16, CH), F32)], axis=0).T
    pos8 = jnp.concatenate([pos, jnp.zeros((5, ATOMS), F32)], axis=0)
    pt = jnp.concatenate([pos8, gpos_t[0:8]], axis=1).astype(BF16)
    own_group = iota((N_GROUP, ATOMS), 1) // GROUP == iota((N_GROUP, ATOMS), 0)
    tile_sel = jnp.where(
        iota((ATOMS, EDGE), 0) % GROUP == iota((ATOMS, EDGE), 1) % GROUP, 1.0, 0.0
    ).astype(BF16)
    for g in range(N_GROUP):
        got = dot(pt, oh_ref[g], NT)
        for c in range(3):
            xyz_ref[c, g : g + 1, :] = got[c : c + 1, :]
    rel = []
    for c in range(3):
        mine = jnp.where(own_group, pos[c : c + 1, :], 0.0).astype(BF16)
        rel.append(xyz_ref[c] - dot(mine, tile_sel))
    d, ux, uy, uz = geometry(*rel)
    for m, val in enumerate(harmonics(ux, uy, uz)):
        ys_ref[:, m, :] = val
    for b, val in enumerate(radial_funs(d)):
        bas_ref[:, b, :] = val
    mask8 = jnp.where(iota((GROUP, EDGE), 1) % GROUP == iota((GROUP, EDGE), 0), 1.0, 0.0)
    w_in = w_in_ref[...]
    scale = 1.0 / math.sqrt(FAN)

    def one_chunk(ch, carry):
        base = ch * CHUNK
        hot = oh_ref[pl.ds(base, CHUNK)].reshape(CHUNK * EDGE, MAXN)
        first = dot(hot, f_ref[:, 0:CH]).reshape(CHUNK, EDGE, CH)
        for q in range(CHUNK):
            h = dot(bas_ref[base + q].astype(BF16), w_in, TN)
            h = (h * jax.nn.sigmoid(h)).astype(BF16)
            rad = dot(h, w_out_ref[...])
            r_ref[q] = rad[:, 0 : DEG * CH]
            y = ys_ref[base + q]
            for l in range(DEG):
                lo = l * l
                cross = rad[:, (DEG + l) * CH : (DEG + l + 1) * CH] * first[q]
                rows = [y[m : m + 1, :] * mask8 for m in range(lo, lo + 2 * l + 1)]
                rows.append(jnp.zeros((GROUP, EDGE), F32))
                lhs = jnp.concatenate(rows, axis=0).astype(BF16)
                got = dot(lhs, cross.astype(BF16))
                for j in range(2 * l + 1):
                    m = lo + j
                    agg_ref[base + q, :, m * CH : (m + 1) * CH] = got[
                        j * GROUP : (j + 1) * GROUP, :
                    ]
        for m in range(0, COMP, 2):
            comps = [m] + ([m + 1] if m + 1 < COMP else [])
            got = dot(hot, f_ref[:, m * CH : (m + len(comps)) * CH])
            for j, mm in enumerate(comps):
                l = degree_of(mm)
                part = got[:, j * CH : (j + 1) * CH].reshape(CHUNK, FAN, GROUP, CH)
                rad = r_ref[:, :, l * CH : (l + 1) * CH].reshape(CHUNK, FAN, GROUP, CH)
                lanes = slice(mm * CH, (mm + 1) * CH)
                agg_ref[pl.ds(base, CHUNK), :, lanes] = agg_ref[
                    pl.ds(base, CHUNK), :, lanes
                ] + jnp.sum(part * rad, axis=1)
        return carry

    lax.fori_loop(0, N_GROUP // CHUNK, one_chunk, 0)

    scale = 1.0 / math.sqrt(FAN)

    def agg_of(m):
        return (agg_ref[:, :, m * CH : (m + 1) * CH].reshape(ATOMS, CH) * scale).astype(BF16)

    gates = jax.nn.sigmoid(dot(agg_of(0), w_gate_ref[...]))
    lane_slot = iota((ATOMS, CH), 1) // N_FUN
    halves = [jnp.zeros((ATOMS, CH), F32), jnp.zeros((ATOMS, CH), F32)]
    for l in range(DEG):
        w_cat = jnp.concatenate([w_mix_ref[l], w_self_ref[l]], axis=0)
        w_r = jnp.concatenate([w_read_ref[:, l, :].astype(F32)] * 16, axis=0).astype(BF16)
        for m in range(l * l, (l + 1) * (l + 1)):
            emb = f_ref[0:ATOMS, m * CH : (m + 1) * CH]
            mixed = dot(jnp.concatenate([agg_of(m), emb], axis=1), w_cat)
            if l == 0:
                add = mixed * jax.nn.sigmoid(mixed)
            else:
                add = mixed * gates[:, (l - 1) * CH : l * CH]
            upd = (emb.astype(F32) + add).astype(BF16)
            upd_ref[m] = upd
            coef = dot(upd, w_r, NT)
            halves[m // 16] = halves[m // 16] + jnp.where(lane_slot == m % 16, coef, 0.0)
    put = jnp.where(iota((8, CH), 1) == iota((8, CH), 0) + 72, 1.0, 0.0).astype(BF16)
    halves[1] = jnp.where(
        lane_slot == 9, dot(pos8.astype(BF16), put, TN), halves[1]
    )
    r_col = jnp.broadcast_to(routes_ref[...].astype(F32), (ATOMS, ATOMS))
    r_row = r_col.T
    before = iota((ATOMS, ATOMS), 0) < iota((ATOMS, ATOMS), 1)
    rank = jnp.sum(
        jnp.where(before, jnp.where(r_col == r_row, 1.0, 0.0), 0.0), axis=0, keepdims=True
    )
    target = (r_row[0:1, :] * 4.0 + rank * 2.0).astype(jnp.int32)
    row = iota((512, ATOMS), 0)
    place = jnp.concatenate(
        [jnp.where(row == target, 1.0, 0.0), jnp.where(row == target + 1, 1.0, 0.0)], axis=1
    ).astype(BF16)
    coefs = jnp.concatenate(halves, axis=0)
    high = coefs.astype(BF16)
    low = (coefs - high.astype(F32)).astype(BF16)
    send_ref[...] = dot(place, high) + dot(place, low)


def atom_call(ci, nbr, routes, pos, feats, ghost, table, w_in, w_out, w_mix, w_self, w_gate, w_read):
    vm = pl.BlockSpec(memory_space=pltpu.VMEM)
    return pl.pallas_call(
        atom_kernel,
        out_shape=(
            jax.ShapeDtypeStruct((COMP, ATOMS, CH), BF16),
            jax.ShapeDtypeStruct((512, CH), F32),
        ),
        in_specs=[pl.BlockSpec(memory_space=pltpu.SMEM)] + [vm] * 12,
        out_specs=(vm, vm),
        scratch_shapes=[
            pltpu.VMEM((MAXN, COMP * CH), BF16),
            pltpu.VMEM((N_GROUP, EDGE, MAXN), BF16),
            pltpu.VMEM((3, N_GROUP, EDGE), F32),
            pltpu.VMEM((N_GROUP, COMP, EDGE), F32),
            pltpu.VMEM((N_GROUP, N_FUN, EDGE), F32),
            pltpu.VMEM((CHUNK, EDGE, DEG * CH), F32),
            pltpu.VMEM((N_GROUP, GROUP, COMP * CH), F32),
        ],
        name="atoms",
    )(ci, nbr, routes, pos, feats, ghost, table, w_in, w_out, w_mix, w_self, w_gate, w_read)


PROBES = 256
SLOTS = 256


def density_kernel(probe_ref, pat_ref, recv_ref, out_ref, ct_ref, px_ref, keep_ref, tot_ref):
    for h in range(2):
        ct_ref[h * CH : (h + 1) * CH, :] = recv_ref[pl.ds(h, SLOTS, stride=2), :].T
    px = jnp.concatenate([probe_ref[...], jnp.zeros((5, PROBES), F32)], axis=0)
    px_ref[...] = px.T
    pat = pat_ref[...].astype(F32).astype(BF16)
    spread = jnp.where(
        iota((SLOTS // 2, SLOTS), 0) == iota((SLOTS // 2, SLOTS), 1) // 2, 1.0, 0.0
    ).astype(BF16)
    keep_ref[...] = dot(pat, spread) * (1.0 / math.sqrt(SLOTS))
    rows = 16

    def block(i, carry):
        start = pl.multiple_of(i * rows, rows)
        p = px_ref[pl.ds(start, rows), :]
        rel = [p[:, c : c + 1] - ct_ref[200 + c : 201 + c, :] for c in range(3)]
        d, ux, uy, uz = geometry(*rel)
        total = [None] * N_FUN
        for m, val in enumerate(harmonics(ux, uy, uz)):
            for b in range(N_FUN):
                term = val * ct_ref[m * N_FUN + b : m * N_FUN + b + 1, :]
                total[b] = term if m == 0 else total[b] + term
        out = None
        for b, phi in enumerate(radial_funs(d)):
            out = phi * total[b] if out is None else out + phi * total[b]
        out = out * keep_ref[pl.ds(i // (PROBES // 2 // rows), 1), :]
        tot_ref[pl.ds(start, rows), :] = jnp.broadcast_to(
            jnp.sum(out, axis=1, keepdims=True), (rows, CH)
        )
        return carry

    lax.fori_loop(0, PROBES // rows, block, 0)
    for h in range(2):
        out_ref[h : h + 1, :] = tot_ref[h * CH : (h + 1) * CH, :].T[0:1, :]


def density_call(probes, pattern, recv):
    vm = pl.BlockSpec(memory_space=pltpu.VMEM)
    return pl.pallas_call(
        density_kernel,
        out_shape=jax.ShapeDtypeStruct((2, CH), F32),
        in_specs=[vm] * 3,
        out_specs=vm,
        scratch_shapes=[
            pltpu.VMEM((2 * CH, SLOTS), F32),
            pltpu.VMEM((PROBES, 8), F32),
            pltpu.VMEM((2, SLOTS), F32),
            pltpu.VMEM((PROBES, CH), F32),
        ],
        name="density",
    )(probes, pattern, recv)


MESH = pl.DeviceIdType.MESH


def halo_kernel(src_ref, dst_ref, send_sem, recv_sem, own_sem):
    gx, gy, gz = lax.axis_index("gx"), lax.axis_index("gy"), lax.axis_index("gz")
    nx, ny, nz = lax.axis_size("gx"), lax.axis_size("gy"), lax.axis_size("gz")
    peers = []
    for n in range(27):
        a, b, c = n // 9 - 1, n // 3 % 3 - 1, n % 3 - 1
        peers.append(
            (
                lax.rem(gx - a + nx, nx),
                lax.rem(gy - b + ny, ny),
                lax.rem(gz - c + nz, nz),
            )
        )
    barrier = pltpu.get_barrier_semaphore()
    for n in range(27):
        if n != 13:
            pl.semaphore_signal(barrier, inc=1, device_id=peers[n], device_id_type=MESH)
    pl.semaphore_wait(barrier, 26)
    copies = []
    for n in range(27):
        if n == 13:
            continue
        copy = pltpu.make_async_remote_copy(
            src_ref=src_ref,
            dst_ref=dst_ref.at[:, n],
            send_sem=send_sem.at[n],
            recv_sem=recv_sem.at[n],
            device_id=peers[n],
            device_id_type=MESH,
        )
        copy.start()
        copies.append(copy)
    own = pltpu.make_async_copy(src_ref, dst_ref.at[:, 13], own_sem)
    own.start()
    own.wait()
    for copy in copies:
        copy.wait()


def halo_call(front):
    vm = pl.BlockSpec(memory_space=pltpu.VMEM)
    return pl.pallas_call(
        halo_kernel,
        out_shape=jax.ShapeDtypeStruct((COMP + 1, 28, 4, CH), BF16),
        in_specs=[vm],
        out_specs=vm,
        scratch_shapes=[
            pltpu.SemaphoreType.DMA((27,)),
            pltpu.SemaphoreType.DMA((27,)),
            pltpu.SemaphoreType.DMA,
        ],
        compiler_params=pltpu.CompilerParams(collective_id=0, has_side_effects=True),
        name="halo",
    )(front)


def tiles_kernel(src_ref, dst_ref, send_sem, recv_sem, own_sem):
    gx, gy, gz = lax.axis_index("gx"), lax.axis_index("gy"), lax.axis_index("gz")
    ny, nz = lax.axis_size("gy"), lax.axis_size("gz")
    count = ny * nz
    me = gy * nz + gz
    barrier = pltpu.get_barrier_semaphore()

    def greet(j, carry):
        t = lax.rem(me + j, count)
        pl.semaphore_signal(
            barrier, inc=1, device_id=(gx, t // nz, lax.rem(t, nz)), device_id_type=MESH
        )
        return carry

    lax.fori_loop(1, count, greet, 0)
    pl.semaphore_wait(barrier, count - 1)

    def post(j, carry):
        t = lax.rem(me + j, count)
        pltpu.make_async_remote_copy(
            src_ref=src_ref.at[t],
            dst_ref=dst_ref.at[me],
            send_sem=send_sem,
            recv_sem=recv_sem,
            device_id=(gx, t // nz, lax.rem(t, nz)),
            device_id_type=MESH,
        ).start()
        return carry

    lax.fori_loop(1, count, post, 0)
    own = pltpu.make_async_copy(src_ref.at[me], dst_ref.at[me], own_sem)
    own.start()
    own.wait()
    part = pl.ds(0, count - 1)
    pltpu.make_async_copy(src_ref.at[part], dst_ref.at[part], send_sem).wait()
    pltpu.make_async_copy(src_ref.at[part], dst_ref.at[part], recv_sem).wait()


def tiles_call(send):
    vm = pl.BlockSpec(memory_space=pltpu.VMEM)
    return pl.pallas_call(
        tiles_kernel,
        out_shape=jax.ShapeDtypeStruct(send.shape, send.dtype),
        in_specs=[vm],
        out_specs=vm,
        scratch_shapes=[pltpu.SemaphoreType.DMA] * 3,
        compiler_params=pltpu.CompilerParams(collective_id=1, has_side_effects=True),
        name="tiles",
    )(send)


def per_device(
    features, positions, probe_positions, neighbours, routes, pattern, charge_index, charge_table,
    w_radial_in, w_radial_out, w_mix, w_self, w_gate, w_read,
):
    feats = jnp.transpose(features, (1, 0, 2))
    coords = jnp.pad(positions[:, :4].T, ((0, 0), (0, CH - 3)))[None]
    front = jnp.concatenate([feats[:, :4], coords], axis=0)
    ghost = halo_call(front).reshape(COMP + 1, 112, CH)
    upd, send = atom_call(
        charge_index, neighbours, routes, positions, feats, ghost, charge_table, w_radial_in,
        w_radial_out, w_mix, w_self, w_gate, w_read,
    )
    recv = tiles_call(send.reshape(128, 4, CH)).reshape(512, CH)
    density = density_call(probe_positions, pattern, recv)
    return jnp.transpose(upd, (1, 0, 2)), density.reshape(PROBES)


def solution(mesh):
    split = ("gx", "gy", "gz")
    rows = P(split, None)
    in_specs = (
        (P(split, None, None), P(None, split), P(None, split), rows, rows, rows) + (P(),) * 8
    )
    out_specs = (P(split, None, None), P(split))
    return jax.shard_map(
        per_device, mesh=mesh, in_specs=in_specs, out_specs=out_specs, check_vma=False
    )
```

time: 503 us -> 79.8 us (0.16)
  other arithmetic: 226 us -> 0.63 us
  local copies, waits for them, and re-layouts: 118 us -> 3.75 us
  Pallas kernels: 0 us -> 73.6 us
  matrix products: 56.9 us -> 0 us
  starting transfers between devices: 50.7 us -> 0 us
  waiting for transfers between devices: 40.1 us -> 0 us
  loops' own time: 5.25 us -> 0 us
    while x238 -> x0, other arithmetic: 155 us -> none
    pallas_call x0 -> x4, Pallas kernels: none -> 73.6 us  [the longest x1 22 us: halo_call(): pl.pallas_call(halo_kernel, out_shape=jax.ShapeDtypeStruct((COMP + 1, 28,...]
    dot_general x86 -> x0, matrix products: 56.9 us -> none  [the longest x25 24.7 us: update_flat(): jnp.dot(agg_part, w_mix[degree], preferred_element_type=jnp.float32)]
    reshape x35 -> x0, local copies, waits for them, and re-layouts: 43.7 us -> none  [the longest x8 39.7 us: one_block(): message.reshape(block_rows, fanout, components * channels)]
    gather x27 -> x0, local copies, waits for them, and re-layouts: 41.9 us -> none  [the longest x8 29.1 us: one_block(): gathered = jnp.take(feats_all, flat_index, axis=0)]
    all_to_all x2 -> x0, waiting for transfers between devices: 40 us -> none  [the longest x1 40 us: per_device(): lax.all_to_all(outgoing, ('gy', 'gz'), split_axis=0, concat_axis=0, tiled...]
    all_to_all x2 -> x0, starting transfers between devices: 29.9 us -> none  [the longest x1 16.2 us: per_device(): lax.all_to_all(outgoing_pos, ('gy', 'gz'), split_axis=0, concat_axis=0, t...]
    reduce_sum x22 -> x0, other arithmetic: 25.6 us -> none  [the longest x8 24.1 us: one_block(): jnp.sum(message.reshape(block_rows, fanout, components * channels), axis=1)]
  transfers between devices with their start and end apart: 8 -> 0, of which waited for: 2 -> 0; matrix products, arithmetic and copies ran while one was open for 73% -> 0% of each run, Pallas kernels for 0% -> 0%
where the time goes in v1:
time: 79.8 us; the launch traced here: 79.3 us
  Pallas kernels  73.6 us (92%)
  local copies, waits for them, and re-layouts  3.75 us (5%)
  between operations  1.33 us (2%)
    pallas_call x1, Pallas kernels, halo_call(): pl.pallas_call(halo_kernel, out_shape=jax.ShapeDtypeStruct((COMP + 1, 28,...  22 us
    pallas_call x1, Pallas kernels, tiles_call(): pl.pallas_call(tiles_kernel, out_shape=jax.ShapeDtypeStruct(send.shape, s...  21.7 us
    pallas_call x1, Pallas kernels, atom_call(): pl.pallas_call(atom_kernel, out_shape=(jax.ShapeDtypeStruct((COMP, ATOMS,...  20.1 us
    pallas_call x1, Pallas kernels, density_call(): pl.pallas_call(density_kernel, out_shape=jax.ShapeDtypeStruct((2, CH), F3...  9.67 us
    unnamed x10, local copies, waits for them, and re-layouts  2.93 us

profile of v1, /device:TPU:1, one launch (start us, length us, event | category | flops | bytes accessed | tf_op | source)
XLA Modules:
  0.0 79.3 jit_solution(17972343659232609956)
XLA Ops:
  0.6 0.0 copy-start.1
  1.3 0.8 copy.20
  2.1 0.0 copy-done.1
  2.1 0.6 copy.19.w_read_ref
  2.7 0.8 %slice.8 = bf16[25,4,128]{2,1,0:T(4,128)(2,1)S(1)} slice(bf16[25,128,128]{2,1,0:T(8,128)(2,1)} %bitcast.12), slice={[0:25], [0:4], [0:128]} | slice | bytes 51200 | tf_op jit(solution)/shard_map/slice | solution.py:427
  3.5 0.0 copy-start
  3.5 0.6 pad_maximum_fusion.src_ref
  4.2 0.1 copy-done
  4.2 0.0 copy-start.2
  4.2 0.7 copy.17.nbr_ref
  5.0 0.0 copy-done.2
  5.0 0.7 copy.18.routes_ref
  5.7 22.0 %halo.1 = bf16[26,28,4,128]{3,2,1,0:T(4,128)(2,1)} custom-call(bf16[26,4,128]{2,1,0:T(4,128)(2,1)} %pad_maximum_fusion.src_ref), custom_call_target="tpu_custom_call" | custom-call | tf_op jit(solution)/shard_map/halo/pallas_call | solution.py:355
  27.7 20.1 %atoms.1 = (bf16[25,128,128]{2,1,0:T(8,128)(2,1)}, f32[512,128]{1,0:T(8,128)}) custom-call(s32[1]{0:T(128)S(6)} %copy.21.ci_ref, s32[128,20]{1,0:T(8,128)} %copy.17.nbr_ref, s32[128,1]{1,0:T(8,128)} %copy.18.routes_ref, bf16[3,128]{1,0:T(4,128)(2,1)} %pos_ref.1, bf16[25,128,128]{2,1,0:T(8,128)(2,1)} %bitcast.13, bf16[26,112,128]{2,1,0:T(8,128)(2,1)} %bitcast.10, ...), custom_call_target="tpu_custom_call" | custom-call | tf_op jit(solution)/shard_map/atoms/pallas_call | solution.py:233
  47.9 21.7 %tiles.1 = f32[128,4,128]{2,1,0:T(4,128)} custom-call(f32[128,4,128]{2,1,0:T(4,128)} %bitcast.14), custom_call_target="tpu_custom_call" | custom-call | tf_op jit(solution)/shard_map/tiles/pallas_call | solution.py:410
  69.6 9.7 %density.1 = f32[2,128]{1,0:T(2,128)} custom-call(f32[3,256]{1,0:T(4,128)} %probe_ref.1, s32[2,128]{1,0:T(2,128)} %pat_ref.1, f32[512,128]{1,0:T(8,128)} %bitcast.11), custom_call_target="tpu_custom_call" | custom-call | tf_op jit(solution)/shard_map/density/pallas_call | solution.py:296
  (1 shorter events, 0.0 us)
Async XLA Ops:
  0.6 1.5 %copy-start.1 = (bf16[8,5,128]{2,0,1:T(8,128)(2,1)S(1)}, bf16[8,5,128]{2,0,1:T(8,128)(2,1)}, u32[]{:S(2)}) copy-start(bf16[8,5,128]{2,0,1:T(8,128)(2,1)} %param.27) | copy-start | bytes 30724
  3.5 0.7 copy-start
  4.2 0.7 copy-start.2

commit v2 on v1

v2 whole, which is shorter than its diff:
```python
import functools, math
import jax
import jax.numpy as jnp
from jax import lax
from jax.experimental import pallas as pl
from jax.experimental.pallas import tpu as pltpu
from jax.sharding import PartitionSpec as P

F32 = jnp.float32
BF16 = jnp.bfloat16
CUTOFF = 8.0
WIDTH_R = 0.75
REACH = 6.0
FLOOR = 0.25
N_FUN = 8
DEG = 5
COMP = 25
CH = 128
ATOMS = 128
FAN = 20
GROUP = 8
N_GROUP = 16
EDGE = GROUP * FAN
CHUNK = 4
MAXN = 256


def degree_of(component):
    return int(math.isqrt(component))


def harmonics(x, y, z):
    xx, yy, zz = x * x, y * y, z * z
    c = math.sqrt
    return [
        jnp.ones_like(x),
        c(3.0) * y,
        c(3.0) * z,
        c(3.0) * x,
        c(15.0) * x * y,
        c(15.0) * y * z,
        0.5 * c(5.0) * (3.0 * zz - 1.0),
        c(15.0) * x * z,
        0.5 * c(15.0) * (xx - yy),
        c(35.0 / 8.0) * y * (3.0 * xx - yy),
        c(105.0) * x * y * z,
        c(21.0 / 8.0) * y * (5.0 * zz - 1.0),
        0.5 * c(7.0) * z * (5.0 * zz - 3.0),
        c(21.0 / 8.0) * x * (5.0 * zz - 1.0),
        0.5 * c(105.0) * z * (xx - yy),
        c(35.0 / 8.0) * x * (xx - 3.0 * yy),
        1.5 * c(35.0) * x * y * (xx - yy),
        1.5 * c(17.5) * y * z * (3.0 * xx - yy),
        1.5 * c(5.0) * x * y * (7.0 * zz - 1.0),
        1.5 * c(2.5) * y * z * (7.0 * zz - 3.0),
        0.375 * (35.0 * zz * zz - 30.0 * zz + 3.0),
        1.5 * c(2.5) * x * z * (7.0 * zz - 3.0),
        0.75 * c(5.0) * (xx - yy) * (7.0 * zz - 1.0),
        1.5 * c(17.5) * x * z * (xx - 3.0 * yy),
        0.375 * c(35.0) * (xx * xx - 6.0 * xx * yy + yy * yy),
    ]


def radial_funs(d):
    q = d * (1.0 / CUTOFF)
    env = 1.0 - q * q
    env = env * env
    out = []
    for b in range(N_FUN):
        v = (d - b * (REACH / (N_FUN - 1))) * (1.0 / WIDTH_R)
        out.append(jnp.exp(-(v * v)) * env)
    return out


def geometry(dx, dy, dz):
    d = jnp.sqrt(dx * dx + dy * dy + dz * dz)
    inv = 1.0 / jnp.maximum(d, FLOOR)
    return d, dx * inv, dy * inv, dz * inv


def iota(shape, dim):
    return lax.broadcasted_iota(jnp.int32, shape, dim)


def dot(a, b, dims=None):
    if dims is None:
        dims = (((1,), (0,)), ((), ()))
    return lax.dot_general(a, b, dims, preferred_element_type=F32)


NT = (((1,), (1,)), ((), ()))
TN = (((0,), (0,)), ((), ()))


MESH = pl.DeviceIdType.MESH


def atom_kernel(
    ci_ref, nbr_ref, routes_ref, pos_ref, table_ref, w_in_ref, feats_hbm, w_out_hbm, w_mix_hbm,
    w_self_hbm, w_gate_hbm, w_read_hbm, upd_hbm, recv_ref,
    f_ref, e_ref, oh_ref, xyz_ref, ys_ref, bas_ref, r_ref, agg_ref, upd_ref, send_ref,
    w_out_ref, w_mix_ref, w_self_ref, w_gate_ref, w_read_ref,
    load_sem, halo_send, halo_recv, tile_sem, plane_sem,
):
    gx, gy, gz = lax.axis_index("gx"), lax.axis_index("gy"), lax.axis_index("gz")
    nx, ny, nz = lax.axis_size("gx"), lax.axis_size("gy"), lax.axis_size("gz")

    def place(a, b, c):
        return (
            lax.rem(gx + a + nx, nx), lax.rem(gy + b + ny, ny), lax.rem(gz + c + nz, nz)
        )

    peers = [place(1 - n // 9, 1 - n // 3 % 3, 1 - n % 3) for n in range(27)]
    others = [n for n in range(27) if n != 13]
    around = [(b, c) for b in (-1, 0, 1) for c in (-1, 0, 1) if (b, c) != (0, 0)]

    def plane_signal(step):
        for b, c in around:
            pl.semaphore_signal(
                plane_sem.at[step],
                inc=1,
                device_id=place(0, b << step, c << step),
                device_id_type=MESH,
            )

    first = pltpu.make_async_copy(
        feats_hbm.at[:, 0:1], f_ref.at[0:COMP, 0:1], load_sem.at[0]
    )
    first.start()
    barrier = pltpu.get_barrier_semaphore()
    for n in others:
        pl.semaphore_signal(barrier, inc=1, device_id=peers[n], device_id_type=MESH)
    rest = pltpu.make_async_copy(
        feats_hbm.at[:, 1:32], f_ref.at[0:COMP, 1:32], load_sem.at[1]
    )
    loads = [
        pltpu.make_async_copy(src, dst, load_sem.at[2 + i])
        for i, (src, dst) in enumerate(
            (
                (w_out_hbm, w_out_ref),
                (w_mix_hbm, w_mix_ref),
                (w_self_hbm, w_self_ref),
                (w_gate_hbm, w_gate_ref),
                (w_read_hbm, w_read_ref),
            )
        )
    ]
    rest.start()
    for load in loads:
        load.start()
    pos = pos_ref[...].astype(F32)
    pos8 = jnp.concatenate([pos, jnp.zeros((5, ATOMS), F32)], axis=0)
    eye = jnp.where(iota((8, CH), 1) == iota((8, CH), 0), 1.0, 0.0).astype(BF16)
    f_ref[COMP, 0] = dot(pos8.astype(BF16), eye, TN)[0:4].astype(BF16)
    f_ref[:, 59:64] = jnp.zeros((COMP + 1, 5, 4, CH), BF16)
    first.wait()
    pl.semaphore_wait(barrier, 26)
    halo = []
    for n in others:
        copy = pltpu.make_async_remote_copy(
            src_ref=f_ref.at[:, 0],
            dst_ref=f_ref.at[:, 32 + n],
            send_sem=halo_send.at[n],
            recv_sem=halo_recv.at[n],
            device_id=peers[n],
            device_id_type=MESH,
        )
        copy.start()
        halo.append(copy)
    mine = pltpu.make_async_copy(f_ref.at[:, 0], f_ref.at[:, 45], load_sem.at[7])
    mine.start()
    plane_signal(0)
    nbr = jnp.concatenate(
        [nbr_ref[...].astype(F32), jnp.zeros((4, ATOMS), F32)], axis=0
    ).T
    col = iota((ATOMS, MAXN), 1).astype(F32)
    for k in range(0, FAN, 2):
        halves = []
        for kk in (k, k + 1):
            hot = jnp.where(nbr[:, kk : kk + 1] == col, 1.0, 0.0)
            halves.append(hot.reshape(N_GROUP, GROUP, MAXN))
        oh_ref[:, k * GROUP : (k + 2) * GROUP, :] = jnp.concatenate(halves, axis=1).astype(BF16)
    lvl = iota((8, CH), 0)
    shift = jnp.sum(
        jnp.where(lvl == ci_ref[0], table_ref[...].astype(F32), 0.0), axis=0, keepdims=True
    )
    flat = f_ref.reshape(COMP + 1, MAXN, CH)
    rest.wait()
    mine.wait()
    for copy in halo:
        copy.wait()
    pl.semaphore_wait(plane_sem.at[0], 8)
    plane_signal(1)
    for load in loads:
        load.wait()
    e_ref[...] = (flat[0].astype(F32) + shift).astype(BF16)
    gpos_t = flat[COMP, ATOMS:MAXN].astype(F32).T
    pt = jnp.concatenate([pos8, gpos_t[0:8]], axis=1).astype(BF16)

    def comp(m):
        return e_ref[...] if m == 0 else flat[m]

    own_group = iota((N_GROUP, ATOMS), 1) // GROUP == iota((N_GROUP, ATOMS), 0)
    tile_sel = jnp.where(
        iota((ATOMS, EDGE), 0) % GROUP == iota((ATOMS, EDGE), 1) % GROUP, 1.0, 0.0
    ).astype(BF16)
    for g in range(N_GROUP):
        got = dot(pt, oh_ref[g], NT)
        for c in range(3):
            xyz_ref[c, g : g + 1, :] = got[c : c + 1, :]
    rel = []
    for c in range(3):
        mine = jnp.where(own_group, pos[c : c + 1, :], 0.0).astype(BF16)
        rel.append(xyz_ref[c] - dot(mine, tile_sel))
    d, ux, uy, uz = geometry(*rel)
    for m, val in enumerate(harmonics(ux, uy, uz)):
        ys_ref[:, m, :] = val
    for b, val in enumerate(radial_funs(d)):
        bas_ref[:, b, :] = val
    mask8 = jnp.where(iota((GROUP, EDGE), 1) % GROUP == iota((GROUP, EDGE), 0), 1.0, 0.0)
    w_in = w_in_ref[...]
    scale = 1.0 / math.sqrt(FAN)

    def one_chunk(ch, carry):
        base = ch * CHUNK
        hot = oh_ref[pl.ds(base, CHUNK)].reshape(CHUNK * EDGE, MAXN)
        scalars = dot(hot, comp(0)).reshape(CHUNK, EDGE, CH)
        for q in range(CHUNK):
            h = dot(bas_ref[base + q].astype(BF16), w_in, TN)
            h = (h * jax.nn.sigmoid(h)).astype(BF16)
            rad = dot(h, w_out_ref[...])
            r_ref[q] = rad[:, 0 : DEG * CH]
            y = ys_ref[base + q]
            for l in range(DEG):
                lo = l * l
                cross = rad[:, (DEG + l) * CH : (DEG + l + 1) * CH] * scalars[q]
                rows = [y[m : m + 1, :] * mask8 for m in range(lo, lo + 2 * l + 1)]
                rows.append(jnp.zeros((GROUP, EDGE), F32))
                lhs = jnp.concatenate(rows, axis=0).astype(BF16)
                got = dot(lhs, cross.astype(BF16))
                for j in range(2 * l + 1):
                    m = lo + j
                    agg_ref[base + q, :, m * CH : (m + 1) * CH] = got[
                        j * GROUP : (j + 1) * GROUP, :
                    ]
        for m in range(0, COMP, 2):
            comps = [m] + ([m + 1] if m + 1 < COMP else [])
            got = dot(hot, jnp.concatenate([comp(mm) for mm in comps], axis=1))
            for j, mm in enumerate(comps):
                l = degree_of(mm)
                part = got[:, j * CH : (j + 1) * CH].reshape(CHUNK, FAN, GROUP, CH)
                rad = r_ref[:, :, l * CH : (l + 1) * CH].reshape(CHUNK, FAN, GROUP, CH)
                lanes = slice(mm * CH, (mm + 1) * CH)
                agg_ref[pl.ds(base, CHUNK), :, lanes] = agg_ref[
                    pl.ds(base, CHUNK), :, lanes
                ] + jnp.sum(part * rad, axis=1)
        return carry

    lax.fori_loop(0, N_GROUP // CHUNK, one_chunk, 0)

    pl.semaphore_wait(plane_sem.at[1], 8)
    plane_signal(2)

    scale = 1.0 / math.sqrt(FAN)

    def agg_of(m):
        return (agg_ref[:, :, m * CH : (m + 1) * CH].reshape(ATOMS, CH) * scale).astype(BF16)

    gates = jax.nn.sigmoid(dot(agg_of(0), w_gate_ref[...]))
    lane_slot = iota((ATOMS, CH), 1) // N_FUN
    halves = [jnp.zeros((ATOMS, CH), F32), jnp.zeros((ATOMS, CH), F32)]
    for l in range(DEG):
        w_cat = jnp.concatenate([w_mix_ref[l], w_self_ref[l]], axis=0)
        w_r = jnp.concatenate([w_read_ref[l].astype(F32)] * 16, axis=0).astype(BF16)
        for m in range(l * l, (l + 1) * (l + 1)):
            emb = comp(m)[0:ATOMS]
            mixed = dot(jnp.concatenate([agg_of(m), emb], axis=1), w_cat)
            if l == 0:
                add = mixed * jax.nn.sigmoid(mixed)
            else:
                add = mixed * gates[:, (l - 1) * CH : l * CH]
            upd = (emb.astype(F32) + add).astype(BF16)
            upd_ref[m] = upd
            coef = dot(upd, w_r, NT)
            halves[m // 16] = halves[m // 16] + jnp.where(lane_slot == m % 16, coef, 0.0)
    put = jnp.where(iota((8, CH), 1) == iota((8, CH), 0) + 72, 1.0, 0.0).astype(BF16)
    halves[1] = jnp.where(
        lane_slot == 9, dot(pos8.astype(BF16), put, TN), halves[1]
    )
    store = pltpu.make_async_copy(upd_ref, upd_hbm, load_sem.at[8])
    store.start()
    r_row = jnp.broadcast_to(routes_ref[...].astype(F32), (ATOMS, ATOMS))
    r_col = r_row.T
    before = iota((ATOMS, ATOMS), 0) < iota((ATOMS, ATOMS), 1)
    rank = jnp.sum(
        jnp.where(before, jnp.where(r_col == r_row, 1.0, 0.0), 0.0), axis=0, keepdims=True
    )
    target = (r_row[0:1, :] * 4.0 + rank * 2.0).astype(jnp.int32)
    row = iota((512, ATOMS), 0)
    put_rows = jnp.concatenate(
        [jnp.where(row == target, 1.0, 0.0), jnp.where(row == target + 1, 1.0, 0.0)], axis=1
    ).astype(BF16)
    coefs = jnp.concatenate(halves, axis=0)
    high = coefs.astype(BF16)
    low = (coefs - high.astype(F32)).astype(BF16)
    send_ref[...] = (dot(put_rows, high) + dot(put_rows, low)).reshape(128, 4, CH)
    pl.semaphore_wait(plane_sem.at[2], 8)
    count = ny * nz
    me = gy * nz + gz

    def post(j, carry):
        t = lax.rem(me + j, count)
        pltpu.make_async_remote_copy(
            src_ref=send_ref.at[t],
            dst_ref=recv_ref.at[me],
            send_sem=tile_sem.at[0],
            recv_sem=tile_sem.at[1],
            device_id=(gx, t // nz, lax.rem(t, nz)),
            device_id_type=MESH,
        ).start()
        return carry

    lax.fori_loop(1, count, post, 0)
    own = pltpu.make_async_copy(send_ref.at[me], recv_ref.at[me], tile_sem.at[2])
    own.start()
    own.wait()
    store.wait()
    part = pl.ds(0, count - 1)
    pltpu.make_async_copy(send_ref.at[part], recv_ref.at[part], tile_sem.at[0]).wait()
    pltpu.make_async_copy(send_ref.at[part], recv_ref.at[part], tile_sem.at[1]).wait()


def atom_call(ci, nbr, routes, pos, table, w_in, feats, w_out, w_mix, w_self, w_gate, w_read):
    vm = pl.BlockSpec(memory_space=pltpu.VMEM)
    hbm = pl.BlockSpec(memory_space=pl.ANY)
    return pl.pallas_call(
        atom_kernel,
        out_shape=(
            jax.ShapeDtypeStruct((COMP, ATOMS, CH), BF16),
            jax.ShapeDtypeStruct((128, 4, CH), F32),
        ),
        in_specs=[pl.BlockSpec(memory_space=pltpu.SMEM)] + [vm] * 5 + [hbm] * 6,
        out_specs=(hbm, hbm),
        scratch_shapes=[
            pltpu.VMEM((COMP + 1, 64, 4, CH), BF16),
            pltpu.VMEM((MAXN, CH), BF16),
            pltpu.VMEM((N_GROUP, EDGE, MAXN), BF16),
            pltpu.VMEM((3, N_GROUP, EDGE), F32),
            pltpu.VMEM((N_GROUP, COMP, EDGE), F32),
            pltpu.VMEM((N_GROUP, N_FUN, EDGE), F32),
            pltpu.VMEM((CHUNK, EDGE, DEG * CH), F32),
            pltpu.VMEM((N_GROUP, GROUP, COMP * CH), F32),
            pltpu.VMEM((COMP, ATOMS, CH), BF16),
            pltpu.VMEM((128, 4, CH), F32),
            pltpu.VMEM((64, 2 * DEG * CH), BF16),
            pltpu.VMEM((DEG, CH, CH), BF16),
            pltpu.VMEM((DEG, CH, CH), BF16),
            pltpu.VMEM((CH, (DEG - 1) * CH), BF16),
            pltpu.VMEM((DEG, N_FUN, CH), BF16),
            pltpu.SemaphoreType.DMA((9,)),
            pltpu.SemaphoreType.DMA((27,)),
            pltpu.SemaphoreType.DMA((27,)),
            pltpu.SemaphoreType.DMA((3,)),
            pltpu.SemaphoreType.REGULAR((3,)),
        ],
        compiler_params=pltpu.CompilerParams(collective_id=0, has_side_effects=True),
        name="atoms",
    )(ci, nbr, routes, pos, table, w_in, feats, w_out, w_mix, w_self, w_gate, w_read)


PROBES = 256
SLOTS = 256


def density_kernel(
    probe_ref, pat_ref, recv_ref, upd_hbm, out_ref, atoms_hbm,
    ct_ref, px_ref, keep_ref, tot_ref, upd_ref, sem,
):
    take = pltpu.make_async_copy(upd_hbm, upd_ref, sem.at[0])
    give = pltpu.make_async_copy(upd_ref, atoms_hbm, sem.at[1])
    take.start()
    for h in range(2):
        ct_ref[h * CH : (h + 1) * CH, :] = recv_ref[pl.ds(h, SLOTS, stride=2), :].T
    px = jnp.concatenate([probe_ref[...], jnp.zeros((5, PROBES), F32)], axis=0)
    px_ref[...] = px.T
    pat = pat_ref[...].astype(F32).astype(BF16)
    spread = jnp.where(
        iota((SLOTS // 2, SLOTS), 0) == iota((SLOTS // 2, SLOTS), 1) // 2, 1.0, 0.0
    ).astype(BF16)
    keep_ref[...] = dot(pat, spread) * (1.0 / math.sqrt(SLOTS))
    rows = 16

    def block(i, carry):
        start = pl.multiple_of(i * rows, rows)
        p = px_ref[pl.ds(start, rows), :]
        rel = [p[:, c : c + 1] - ct_ref[200 + c : 201 + c, :] for c in range(3)]
        d, ux, uy, uz = geometry(*rel)
        total = [None] * N_FUN
        for m, val in enumerate(harmonics(ux, uy, uz)):
            for b in range(N_FUN):
                term = val * ct_ref[m * N_FUN + b : m * N_FUN + b + 1, :]
                total[b] = term if m == 0 else total[b] + term
        out = None
        for b, phi in enumerate(radial_funs(d)):
            out = phi * total[b] if out is None else out + phi * total[b]
        out = out * keep_ref[pl.ds(i // (PROBES // 2 // rows), 1), :]
        tot_ref[pl.ds(start, rows), :] = jnp.broadcast_to(
            jnp.sum(out, axis=1, keepdims=True), (rows, CH)
        )
        return carry

    steps = PROBES // rows
    lax.fori_loop(0, steps // 4, block, 0)
    take.wait()
    give.start()
    lax.fori_loop(steps // 4, steps, block, 0)
    for h in range(2):
        out_ref[h : h + 1, :] = tot_ref[h * CH : (h + 1) * CH, :].T[0:1, :]
    give.wait()


def density_call(probes, pattern, recv, upd):
    vm = pl.BlockSpec(memory_space=pltpu.VMEM)
    hbm = pl.BlockSpec(memory_space=pl.ANY)
    return pl.pallas_call(
        density_kernel,
        out_shape=(
            jax.ShapeDtypeStruct((2, CH), F32),
            jax.ShapeDtypeStruct((COMP, ATOMS, CH), BF16),
        ),
        in_specs=[vm] * 3 + [hbm],
        out_specs=(vm, hbm),
        scratch_shapes=[
            pltpu.VMEM((2 * CH, SLOTS), F32),
            pltpu.VMEM((PROBES, 8), F32),
            pltpu.VMEM((2, SLOTS), F32),
            pltpu.VMEM((PROBES, CH), F32),
            pltpu.VMEM((COMP, ATOMS, CH), BF16),
            pltpu.SemaphoreType.DMA((2,)),
        ],
        name="density",
    )(probes, pattern, recv, upd)


def per_device(
    features, positions, probe_positions, neighbours, routes, pattern, charge_index, charge_table,
    w_radial_in, w_radial_out, w_mix, w_self, w_gate, w_read,
):
    feats = jnp.transpose(features, (1, 0, 2)).reshape(COMP, 32, 4, CH)
    upd, recv = atom_call(
        charge_index, neighbours.T, routes.T, positions, charge_table, w_radial_in, feats,
        w_radial_out, w_mix, w_self, w_gate, jnp.transpose(w_read, (1, 0, 2)),
    )
    density, atoms = density_call(probe_positions, pattern, recv.reshape(512, CH), upd)
    return jnp.transpose(atoms, (1, 0, 2)), density.reshape(PROBES)


def solution(mesh):
    split = ("gx", "gy", "gz")
    rows = P(split, None)
    in_specs = (
        (P(split, None, None), P(None, split), P(None, split), rows, rows, rows) + (P(),) * 8
    )
    out_specs = (P(split, None, None), P(split))
    return jax.shard_map(
        per_device, mesh=mesh, in_specs=in_specs, out_specs=out_specs, check_vma=False
    )
```

time: 79.8 us -> 62.6 us (0.78)
  Pallas kernels: 73.6 us -> 61.1 us
  local copies, waits for them, and re-layouts: 3.75 us -> 0 us
    pallas_call x3 -> x1, Pallas kernels: 53.4 us -> 9.68 us  [density_call(): pl.pallas_call(density_kernel, out_shape=(jax.ShapeDtypeStruct((2, CH), F...]
    pallas_call x1, Pallas kernels: 20.1 us -> 51.4 us  [atom_call(): pl.pallas_call(atom_kernel, out_shape=(jax.ShapeDtypeStruct((COMP, ATOMS,...]
    unnamed x10 -> x0, local copies, waits for them, and re-layouts: 2.93 us -> none
    slice x1 -> x0, local copies, waits for them, and re-layouts: 0.81 us -> none  [per_device(): front = jnp.concatenate([feats[:, :4], coords], axis=0)]
where the time goes in v2:
time: 62.6 us; the launch traced here: 62.4 us
  Pallas kernels  61.1 us (98%)
  between operations  1.29 us (2%)
    pallas_call x1, Pallas kernels, atom_call(): pl.pallas_call(atom_kernel, out_shape=(jax.ShapeDtypeStruct((COMP, ATOMS,...  51.4 us
    pallas_call x1, Pallas kernels, density_call(): pl.pallas_call(density_kernel, out_shape=(jax.ShapeDtypeStruct((2, CH), F...  9.68 us

profile of v2, /device:TPU:1, one launch (start us, length us, event | category | flops | bytes accessed | tf_op | source)
XLA Modules:
  0.0 62.4 jit_solution(11191965099959633026)
XLA Ops:
  1.3 51.4 %atoms.1 = (bf16[25,128,128]{2,1,0:T(8,128)(2,1)}, f32[128,4,128]{2,1,0:T(4,128)}) custom-call(s32[1]{0:T(128)S(6)} %copy.16.ci_ref, s32[20,128]{1,0:T(8,128)} %bitcast.11, s32[1,128]{1,0:T(1,128)} %bitcast.13, bf16[3,128]{1,0:T(4,128)(2,1)} %pos_ref.1, bf16[8,128]{1,0:T(8,128)(2,1)} %table_ref.1, bf16[8,64]{1,0:T(8,128)(2,1)} %w_in_ref.1, ...), custom_call_target="tpu_custom_call" | custom-call | tf_op jit(solution)/shard_map/atoms/pallas_call | solution.py:336
  52.7 9.7 %density.1 = (f32[2,128]{1,0:T(2,128)}, bf16[25,128,128]{2,1,0:T(8,128)(2,1)}) custom-call(f32[3,256]{1,0:T(4,128)} %probe_ref.1, s32[2,128]{1,0:T(2,128)} %pat_ref.1, f32[512,128]{1,0:T(8,128)} %bitcast.10, bf16[25,128,128]{2,1,0:T(8,128)(2,1)} %get-tuple-element.7.upd_hbm), custom_call_target="tpu_custom_call" | custom-call | tf_op jit(solution)/shard_map/density/pallas_call | solution.py:425

commit v3 on v2

--- a/solution.py
+++ b/solution.py
@@ -93,14 +93,16 @@
 
 
 MESH = pl.DeviceIdType.MESH
+ROW_OF = (0, 16, 48, 96, 160)
+ROWS = 240
 
 
 def atom_kernel(
     ci_ref, nbr_ref, routes_ref, pos_ref, table_ref, w_in_ref, feats_hbm, w_out_hbm, w_mix_hbm,
     w_self_hbm, w_gate_hbm, w_read_hbm, upd_hbm, recv_ref,
-    f_ref, e_ref, oh_ref, xyz_ref, ys_ref, bas_ref, r_ref, agg_ref, upd_ref, send_ref,
-    w_out_ref, w_mix_ref, w_self_ref, w_gate_ref, w_read_ref,
-    load_sem, halo_send, halo_recv, tile_sem, plane_sem,
+    f_ref, e_ref, oh_ref, xyz_ref, ys_ref, bas_ref, y_ref, r_ref, s_ref, agg_ref, cross_ref,
+    upd_ref, send_ref, w_out_ref, w_mix_ref, w_self_ref, w_gate_ref, w_read_ref, spread_ref,
+    load_sem, pos_send, pos_recv, halo_send, halo_recv, tile_sem, plane_sem,
 ):
     gx, gy, gz = lax.axis_index("gx"), lax.axis_index("gy"), lax.axis_index("gz")
     nx, ny, nz = lax.axis_size("gx"), lax.axis_size("gy"), lax.axis_size("gz")
@@ -149,17 +151,30 @@
     for load in loads:
         load.start()
     pos = pos_ref[...].astype(F32)
-    pos8 = jnp.concatenate([pos, jnp.zeros((5, ATOMS), F32)], axis=0)
+    pos8 = jnp.concatenate(
+        [pos, jnp.ones((1, ATOMS), F32), jnp.zeros((4, ATOMS), F32)], axis=0
+    )
     eye = jnp.where(iota((8, CH), 1) == iota((8, CH), 0), 1.0, 0.0).astype(BF16)
     f_ref[COMP, 0] = dot(pos8.astype(BF16), eye, TN)[0:4].astype(BF16)
     f_ref[:, 59:64] = jnp.zeros((COMP + 1, 5, 4, CH), BF16)
     first.wait()
     pl.semaphore_wait(barrier, 26)
-    halo = []
+    sent, halo = [], []
     for n in others:
         copy = pltpu.make_async_remote_copy(
-            src_ref=f_ref.at[:, 0],
-            dst_ref=f_ref.at[:, 32 + n],
+            src_ref=f_ref.at[COMP, 0],
+            dst_ref=f_ref.at[COMP, 32 + n],
+            send_sem=pos_send.at[n],
+            recv_sem=pos_recv.at[n],
+            device_id=peers[n],
+            device_id_type=MESH,
+        )
+        copy.start()
+        sent.append(copy)
+    for n in others:
+        copy = pltpu.make_async_remote_copy(
+            src_ref=f_ref.at[0:COMP, 0],
+            dst_ref=f_ref.at[0:COMP, 32 + n],
             send_sem=halo_send.at[n],
             recv_sem=halo_recv.at[n],
             device_id=peers[n],
@@ -185,21 +200,22 @@
         jnp.where(lvl == ci_ref[0], table_ref[...].astype(F32), 0.0), axis=0, keepdims=True
     )
     flat = f_ref.reshape(COMP + 1, MAXN, CH)
-    rest.wait()
     mine.wait()
-    for copy in halo:
-        copy.wait()
-    pl.semaphore_wait(plane_sem.at[0], 8)
-    plane_signal(1)
     for load in loads:
         load.wait()
-    e_ref[...] = (flat[0].astype(F32) + shift).astype(BF16)
+    spread_ref[...] = jnp.zeros((MAXN, COMP * CH), BF16)
+    none8 = jnp.zeros((N_FUN, CH), F32)
+    for m in range(COMP):
+        one = w_read_ref[degree_of(m)].astype(F32)
+        two = [one, none8] if m % 2 == 0 else [none8, one]
+        start = (m - m % 2) * N_FUN
+        spread_ref[start : start + 16, m * CH : (m + 1) * CH] = jnp.concatenate(
+            two, axis=0
+        ).astype(BF16)
+    for copy in sent:
+        copy.wait()
     gpos_t = flat[COMP, ATOMS:MAXN].astype(F32).T
     pt = jnp.concatenate([pos8, gpos_t[0:8]], axis=1).astype(BF16)
-
-    def comp(m):
-        return e_ref[...] if m == 0 else flat[m]
-
     own_group = iota((N_GROUP, ATOMS), 1) // GROUP == iota((N_GROUP, ATOMS), 0)
     tile_sel = jnp.where(
         iota((ATOMS, EDGE), 0) % GROUP == iota((ATOMS, EDGE), 1) % GROUP, 1.0, 0.0
@@ -210,8 +226,8 @@
             xyz_ref[c, g : g + 1, :] = got[c : c + 1, :]
     rel = []
     for c in range(3):
-        mine = jnp.where(own_group, pos[c : c + 1, :], 0.0).astype(BF16)
-        rel.append(xyz_ref[c] - dot(mine, tile_sel))
+        mine_c = jnp.where(own_group, pos[c : c + 1, :], 0.0).astype(BF16)
+        rel.append(xyz_ref[c] - dot(mine_c, tile_sel))
     d, ux, uy, uz = geometry(*rel)
     for m, val in enumerate(harmonics(ux, uy, uz)):
         ys_ref[:, m, :] = val
@@ -219,59 +235,83 @@
         bas_ref[:, b, :] = val
     mask8 = jnp.where(iota((GROUP, EDGE), 1) % GROUP == iota((GROUP, EDGE), 0), 1.0, 0.0)
     w_in = w_in_ref[...]
-    scale = 1.0 / math.sqrt(FAN)
+    pl.semaphore_wait(plane_sem.at[0], 8)
+    plane_signal(1)
+
+    def radial_chunk(ch, carry):
+        base = ch * CHUNK
+        for q in range(CHUNK):
+            h = dot(bas_ref[base + q].astype(BF16), w_in, TN)
+            h = (h * jax.nn.sigmoid(h)).astype(BF16)
+            r_ref[base + q] = dot(h, w_out_ref[...])
+            y = ys_ref[base + q]
+            for l in range(DEG):
+                lo = l * l
+                rows = [y[m : m + 1, :] * mask8 for m in range(lo, lo + 2 * l + 1)]
+                rows.append(jnp.zeros((GROUP, EDGE), F32))
+                y_ref[base + q, ROW_OF[l] : ROW_OF[l] + (2 * l + 2) * GROUP] = jnp.concatenate(
+                    rows, axis=0
+                ).astype(BF16)
+        return carry
+
+    lax.fori_loop(0, N_GROUP // CHUNK, radial_chunk, 0)
+    rest.wait()
+    for copy in halo:
+        copy.wait()
+    pl.semaphore_wait(plane_sem.at[1], 8)
+    plane_signal(2)
+    e_ref[...] = (flat[0].astype(F32) + shift).astype(BF16)
+
+    def comp(m):
+        return e_ref[...] if m == 0 else flat[m]
+
+    def cross_unit(base, q, l):
+        rad = r_ref[base + q, :, (DEG + l) * CH : (DEG + l + 1) * CH]
+        part = (rad * s_ref[q]).astype(BF16)
+        lhs = y_ref[base + q, ROW_OF[l] : ROW_OF[l] + (2 * l + 2) * GROUP]
+        got = dot(lhs, part)
+        for j in range(2 * l + 1):
+            m = l * l + j
+            cross_ref[base + q, :, m * CH : (m + 1) * CH] = got[j * GROUP : (j + 1) * GROUP, :]
+
+    units = [(q, l) for l in range(DEG) for q in range(CHUNK)]
 
     def one_chunk(ch, carry):
         base = ch * CHUNK
         hot = oh_ref[pl.ds(base, CHUNK)].reshape(CHUNK * EDGE, MAXN)
-        scalars = dot(hot, comp(0)).reshape(CHUNK, EDGE, CH)
-        for q in range(CHUNK):
-            h = dot(bas_ref[base + q].astype(BF16), w_in, TN)
-            h = (h * jax.nn.sigmoid(h)).astype(BF16)
-            rad = dot(h, w_out_ref[...])
-            r_ref[q] = rad[:, 0 : DEG * CH]
-            y = ys_ref[base + q]
-            for l in range(DEG):
-                lo = l * l
-                cross = rad[:, (DEG + l) * CH : (DEG + l + 1) * CH] * scalars[q]
-                rows = [y[m : m + 1, :] * mask8 for m in range(lo, lo + 2 * l + 1)]
-                rows.append(jnp.zeros((GROUP, EDGE), F32))
-                lhs = jnp.concatenate(rows, axis=0).astype(BF16)
-                got = dot(lhs, cross.astype(BF16))
-                for j in range(2 * l + 1):
-                    m = lo + j
-                    agg_ref[base + q, :, m * CH : (m + 1) * CH] = got[
-                        j * GROUP : (j + 1) * GROUP, :
-                    ]
+        todo = list(units)
         for m in range(0, COMP, 2):
             comps = [m] + ([m + 1] if m + 1 < COMP else [])
             got = dot(hot, jnp.concatenate([comp(mm) for mm in comps], axis=1))
+            if m == 0:
+                s_ref[...] = got[:, 0:CH].reshape(CHUNK, EDGE, CH)
+            else:
+                for q, l in todo[:2]:
+                    cross_unit(base, q, l)
+                todo = todo[2:]
             for j, mm in enumerate(comps):
                 l = degree_of(mm)
                 part = got[:, j * CH : (j + 1) * CH].reshape(CHUNK, FAN, GROUP, CH)
-                rad = r_ref[:, :, l * CH : (l + 1) * CH].reshape(CHUNK, FAN, GROUP, CH)
-                lanes = slice(mm * CH, (mm + 1) * CH)
-                agg_ref[pl.ds(base, CHUNK), :, lanes] = agg_ref[
-                    pl.ds(base, CHUNK), :, lanes
-                ] + jnp.sum(part * rad, axis=1)
+                rad = r_ref[pl.ds(base, CHUNK), :, l * CH : (l + 1) * CH].reshape(
+                    CHUNK, FAN, GROUP, CH
+                )
+                agg_ref[pl.ds(base, CHUNK), :, mm * CH : (mm + 1) * CH] = jnp.sum(
+                    part * rad, axis=1
+                )
         return carry
 
     lax.fori_loop(0, N_GROUP // CHUNK, one_chunk, 0)
 
-    pl.semaphore_wait(plane_sem.at[1], 8)
-    plane_signal(2)
-
     scale = 1.0 / math.sqrt(FAN)
 
     def agg_of(m):
-        return (agg_ref[:, :, m * CH : (m + 1) * CH].reshape(ATOMS, CH) * scale).astype(BF16)
+        lanes = slice(m * CH, (m + 1) * CH)
+        both = agg_ref[:, :, lanes] + cross_ref[:, :, lanes]
+        return (both.reshape(ATOMS, CH) * scale).astype(BF16)
 
     gates = jax.nn.sigmoid(dot(agg_of(0), w_gate_ref[...]))
-    lane_slot = iota((ATOMS, CH), 1) // N_FUN
-    halves = [jnp.zeros((ATOMS, CH), F32), jnp.zeros((ATOMS, CH), F32)]
     for l in range(DEG):
         w_cat = jnp.concatenate([w_mix_ref[l], w_self_ref[l]], axis=0)
-        w_r = jnp.concatenate([w_read_ref[l].astype(F32)] * 16, axis=0).astype(BF16)
         for m in range(l * l, (l + 1) * (l + 1)):
             emb = comp(m)[0:ATOMS]
             mixed = dot(jnp.concatenate([agg_of(m), emb], axis=1), w_cat)
@@ -279,16 +319,16 @@
                 add = mixed * jax.nn.sigmoid(mixed)
             else:
                 add = mixed * gates[:, (l - 1) * CH : l * CH]
-            upd = (emb.astype(F32) + add).astype(BF16)
-            upd_ref[m] = upd
-            coef = dot(upd, w_r, NT)
-            halves[m // 16] = halves[m // 16] + jnp.where(lane_slot == m % 16, coef, 0.0)
-    put = jnp.where(iota((8, CH), 1) == iota((8, CH), 0) + 72, 1.0, 0.0).astype(BF16)
-    halves[1] = jnp.where(
-        lane_slot == 9, dot(pos8.astype(BF16), put, TN), halves[1]
-    )
+            upd_ref[m] = (emb.astype(F32) + add).astype(BF16)
     store = pltpu.make_async_copy(upd_ref, upd_hbm, load_sem.at[8])
     store.start()
+    coef = dot(
+        jnp.concatenate([upd_ref[m] for m in range(COMP)], axis=1), spread_ref[...], NT
+    )
+    put = jnp.where(iota((8, CH), 1) == iota((8, CH), 0) + 72, 1.0, 0.0).astype(BF16)
+    coefs = jnp.concatenate(
+        [coef[:, 0:CH], coef[:, CH:] + dot(pos8.astype(BF16), put, TN)], axis=0
+    )
     r_row = jnp.broadcast_to(routes_ref[...].astype(F32), (ATOMS, ATOMS))
     r_col = r_row.T
     before = iota((ATOMS, ATOMS), 0) < iota((ATOMS, ATOMS), 1)
@@ -300,7 +340,6 @@
     put_rows = jnp.concatenate(
         [jnp.where(row == target, 1.0, 0.0), jnp.where(row == target + 1, 1.0, 0.0)], axis=1
     ).astype(BF16)
-    coefs = jnp.concatenate(halves, axis=0)
     high = coefs.astype(BF16)
     low = (coefs - high.astype(F32)).astype(BF16)
     send_ref[...] = (dot(put_rows, high) + dot(put_rows, low)).reshape(128, 4, CH)
@@ -348,7 +387,10 @@
             pltpu.VMEM((3, N_GROUP, EDGE), F32),
             pltpu.VMEM((N_GROUP, COMP, EDGE), F32),
             pltpu.VMEM((N_GROUP, N_FUN, EDGE), F32),
-            pltpu.VMEM((CHUNK, EDGE, DEG * CH), F32),
+            pltpu.VMEM((N_GROUP, ROWS, EDGE), BF16),
+            pltpu.VMEM((N_GROUP, EDGE, 2 * DEG * CH), F32),
+            pltpu.VMEM((CHUNK, EDGE, CH), F32),
+            pltpu.VMEM((N_GROUP, GROUP, COMP * CH), F32),
             pltpu.VMEM((N_GROUP, GROUP, COMP * CH), F32),
             pltpu.VMEM((COMP, ATOMS, CH), BF16),
             pltpu.VMEM((128, 4, CH), F32),
@@ -357,7 +399,10 @@
             pltpu.VMEM((DEG, CH, CH), BF16),
             pltpu.VMEM((CH, (DEG - 1) * CH), BF16),
             pltpu.VMEM((DEG, N_FUN, CH), BF16),
+            pltpu.VMEM((MAXN, COMP * CH), BF16),
             pltpu.SemaphoreType.DMA((9,)),
+            pltpu.SemaphoreType.DMA((27,)),
+            pltpu.SemaphoreType.DMA((27,)),
             pltpu.SemaphoreType.DMA((27,)),
             pltpu.SemaphoreType.DMA((27,)),
             pltpu.SemaphoreType.DMA((3,)),

time: 62.6 us -> 57.1 us (0.912)
  Pallas kernels: 61.1 us -> 55.6 us
    pallas_call x1, Pallas kernels: 51.4 us -> 45.9 us  [atom_call(): pl.pallas_call(atom_kernel, out_shape=(jax.ShapeDtypeStruct((COMP, ATOMS,...]
where the time goes in v3:
time: 57.1 us; the launch traced here: 56.9 us
  Pallas kernels  55.6 us (97%)
  between operations  1.29 us (2%)
    pallas_call x1, Pallas kernels, atom_call(): pl.pallas_call(atom_kernel, out_shape=(jax.ShapeDtypeStruct((COMP, ATOMS,...  45.9 us
    pallas_call x1, Pallas kernels, density_call(): pl.pallas_call(density_kernel, out_shape=(jax.ShapeDtypeStruct((2, CH), F...  9.68 us

profile of v3, /device:TPU:1, one launch (start us, length us, event | category | flops | bytes accessed | tf_op | source)
XLA Modules:
  0.0 56.9 jit_solution(15325382650423615917)
XLA Ops:
  1.3 45.9 %atoms.1 = (bf16[25,128,128]{2,1,0:T(8,128)(2,1)}, f32[128,4,128]{2,1,0:T(4,128)}) custom-call(s32[1]{0:T(128)S(6)} %copy.16.ci_ref, s32[20,128]{1,0:T(8,128)} %bitcast.11, s32[1,128]{1,0:T(1,128)} %bitcast.13, bf16[3,128]{1,0:T(4,128)(2,1)} %pos_ref.1, bf16[8,128]{1,0:T(8,128)(2,1)} %table_ref.1, bf16[8,64]{1,0:T(8,128)(2,1)} %w_in_ref.1, ...), custom_call_target="tpu_custom_call" | custom-call | tf_op jit(solution)/shard_map/atoms/pallas_call | solution.py:375
  47.2 9.7 %density.1 = (f32[2,128]{1,0:T(2,128)}, bf16[25,128,128]{2,1,0:T(8,128)(2,1)}) custom-call(f32[3,256]{1,0:T(4,128)} %probe_ref.1, s32[2,128]{1,0:T(2,128)} %pat_ref.1, f32[512,128]{1,0:T(8,128)} %bitcast.10, bf16[25,128,128]{2,1,0:T(8,128)(2,1)} %get-tuple-element.7.upd_hbm), custom_call_target="tpu_custom_call" | custom-call | tf_op jit(solution)/shard_map/density/pallas_call | solution.py:470
